TPU v7x, 32 devices: a whole 2x2x4 slice. The times are simulated.
32 devices in a mesh: batch: 8 (over z, y), ffn: 4 (over x, core).
Axes of the slice: x: 2, y: 2, z: 4, core: 2. Of those that a mesh axis runs over, the one named last changes fastest.
Arguments:
- tokens: bfloat16 [50112, 768], P(('batch', 'ffn')), may hold values from -6 to 6
- text_lengths: int32 [192], P(('batch', 'ffn')), may hold values from 8 to 64
- routes: int32 [50112, 1], P(('batch', 'ffn')), may hold values from 0 to 7; in each aligned block of 1566 rows (0 to 1565, 1566 to 3131, ...) at most 261 rows name the same one
- group_map: int32 [8], replicated, may hold values from 0 to 2, as said below
- gain_one: float32 [768], replicated, may hold values from 0.1 to 1.9
- w_qkv: bfloat16 [768, 2304], replicated, may hold values from -0.3125 to 0.3125
- w_proj: bfloat16 [768, 768], replicated, may hold values from -0.875 to 0.875
- gain_two: float32 [768], replicated, may hold values from 0.1 to 1.9
- w_in: bfloat16 [8, 768, 3072], P('batch', None, 'ffn'), as said below
- w_back: bfloat16 [8, 3072, 768], P('batch', 'ffn'), as said below
- cotangent: bfloat16 [50112, 768], P(('batch', 'ffn')), may hold values from -6 to 6
Outputs:
- block_out: float32 [50112, 768], P(('batch', 'ffn'))
- input_grad: float32 [50112, 768], P(('batch', 'ffn'))
- grad_gain_one: float32 [768], replicated
- grad_w_qkv: float32 [768, 2304], replicated
- grad_w_proj: float32 [768, 768], replicated
- grad_gain_two: float32 [768], replicated
- grad_w_in: float32 [8, 768, 3072], P('batch', None, 'ffn')
- grad_w_back: float32 [8, 3072, 768], P('batch', 'ffn')
Inputs may be any that keep to these rules, and one draw needn't show every extreme that they name: `routes`: among the rows of one device each index of batch is named by at most 261 rows, and by exactly 261 rows in some devices' rows. `group_map`: every expert is hosted by at least one index of batch; the numbers of indices hosting each expert differ by at most one. w_in[i] equals w_in[j] whenever group_map[i] equals group_map[j]. w_back[i] equals w_back[j] whenever group_map[i] equals group_map[j].
All inputs are finite; a program needn't handle non-finite values.
Results may differ from a plain program's by a relative error of at most 0.015.
The roundings to bfloat16 on the way count: a program that leaves them out, or rounds other values in their place, can miss the bound.
Values may be sent and summed in bfloat16 or wider, within the bound.
A program may use at most 256 MiB of HBM per device.

v0:
```python
import functools
import math

import jax
import jax.numpy as jnp
from jax import lax
from jax.experimental import pallas as pl
from jax.experimental.pallas import tpu as pltpu
from jax.sharding import PartitionSpec as P

D = 768
HEADS = 12
HEAD_DIM = 64
EXPERTS = 3
PATCHES = 197
SEQ_DEV = 6
SEQ_LEN = 261
TOK_DEV = 1566
ROWS = 1584
SORTED = 1616
WIN = 288
TILE = 528
LANES = 1664
EPS = 1e-05
F32 = jnp.float32
BF16 = jnp.bfloat16
I32 = jnp.int32
CONTRACT_LANES = (((1,), (1,)), ((), ()))
CONTRACT_ROWS = (((0,), (0,)), ((), ()))


def params(**extra):
    return pltpu.CompilerParams(vmem_limit_bytes=60 << 20, **extra)


def cost(flops, moved):
    return pl.CostEstimate(flops=int(flops), bytes_accessed=int(moved), transcendentals=0)


def dot(a, b, dims=(((1,), (0,)), ((), ()))):
    return lax.dot_general(a, b, dims, preferred_element_type=F32)


def full(shape):
    zeros = (0,) * len(shape)
    return pl.BlockSpec(shape, lambda *_: zeros)


def once(shape):
    zeros = (0,) * len(shape)
    return pl.BlockSpec(shape, lambda *_: zeros, pipeline_mode=pl.Buffered(1))


def row_mask(start, rows, limit):
    return start + lax.broadcasted_iota(I32, (rows, 1), 0) < limit


def norm_parts(values):
    average = jnp.mean(values, axis=-1, keepdims=True)
    centred = values - average
    variance = jnp.mean(centred * centred, axis=-1, keepdims=True)
    inverse = lax.rsqrt(variance + EPS)
    return centred * inverse, inverse


def norm_pull(grad_normed, gain, normal, inverse):
    scaled = grad_normed * gain
    mean_grad = jnp.mean(scaled, axis=-1, keepdims=True)
    mean_proj = jnp.mean(scaled * normal, axis=-1, keepdims=True)
    return inverse * (scaled - mean_grad - normal * mean_proj)


def route_rows(n_batch, gm_ref, routes_ref, pos_ref, col_ref, offs_ref):
    routes = routes_ref[...]
    lane = lax.broadcasted_iota(I32, (8, LANES), 1)
    sub = lax.broadcasted_iota(I32, (8, LANES), 0)
    expert = jnp.zeros((1, LANES), I32)
    for b in range(n_batch):
        expert = jnp.where(routes == b, gm_ref[b], expert)
    live = lane < TOK_DEV
    hot = jnp.where((jnp.broadcast_to(expert, (8, LANES)) == sub) & live, 1, 0)
    count = hot
    step = 1
    while step < LANES:
        count = count + jnp.where(lane >= step, pltpu.roll(count, step, 1), 0)
        step *= 2
    totals = [jnp.sum(hot[e : e + 1, :], axis=1, keepdims=True) for e in range(EXPERTS)]
    starts = [jnp.zeros((1, 1), I32)]
    for e in range(EXPERTS):
        starts.append(starts[-1] + (totals[e] + 15) // 16 * 16)
    pos = jnp.zeros((1, LANES), I32)
    for e in range(EXPERTS):
        pos = pos + jnp.where(hot[e : e + 1, :] > 0, count[e : e + 1, :] - 1 + starts[e], 0)
    pos = jnp.where(live[0:1, :], pos, -1)
    pos_ref[...] = pos
    wide = jnp.broadcast_to(pos.astype(F32), (128, LANES))
    col_ref[...] = jnp.transpose(wide).astype(I32)
    slot = lax.broadcasted_iota(I32, (1, 128), 1)
    offs = jnp.zeros((1, 128), I32)
    for e in range(EXPERTS + 1):
        offs = jnp.where(slot == e, starts[e], offs)
    offs_ref[...] = offs


SORT_TILES = (336, 336, 336, 336, 272)


def window(pair):
    first = pair * SEQ_LEN
    start = first // 16 * 16
    return start, first - start


def head_cols(hp, part):
    return pl.ds(pl.multiple_of(part * D + hp * 128, 128), 128)


def attend_pair(pair, length, qkv_ref, ctx_ref, lse_ref, stat):
    start, skip = window(pair)
    start = pl.multiple_of(start, 16)
    key = lax.broadcasted_iota(I32, (1, WIN), 1)
    seen = (key >= skip) & (key < skip + PATCHES + length)
    bias = jnp.where(seen, 0.0, -1e30)
    row = lax.broadcasted_iota(I32, (WIN, 1), 0)
    mine = (row >= skip) & (row < skip + SEQ_LEN)
    lane = lax.broadcasted_iota(I32, (WIN, 128), 1)
    stat[...] = jnp.zeros_like(stat)
    @pl.loop(0, HEADS // 2)
    def _(hp):
        q, k, v = [qkv_ref[pl.ds(start, WIN), head_cols(hp, part)] for part in range(3)]
        cols = head_cols(hp, 0)
        q = q * jnp.asarray(HEAD_DIM**-0.5, BF16)
        pieces = []
        for half in range(2):
            inside = (lane < 64) if half == 0 else (lane >= 64)
            qh = jnp.where(inside, q, jnp.zeros_like(q))
            scores = dot(qh, k, CONTRACT_LANES) + bias
            peak = jnp.max(scores, axis=1, keepdims=True)
            weight = jnp.exp(scores - peak).astype(BF16)
            vh = jnp.where(inside, v, jnp.ones_like(v))
            mixed = dot(weight, vh)
            total = pltpu.roll(mixed, 64, 1)
            pieces.append(mixed / total)
            one = total[:, 0:1] if half == 0 else mixed[:, 0:1]
            head = hp * 2 + half
            stat[0:WIN, :] = jnp.where(lane == head, peak + jnp.log(one), stat[0:WIN, :])
        ctx = jnp.where(lane < 64, pieces[0], pieces[1]).astype(BF16)
        old = ctx_ref[pl.ds(start, WIN), cols]
        ctx_ref[pl.ds(start, WIN), cols] = jnp.where(mine, ctx, old)
    lse_ref[pair] = jnp.transpose(stat[...])[0:16, :]


MESH = pl.DeviceIdType.MESH
HALF = 384
FF_DEV = 768
HOPS = [(way, hop) for hop in (1, 2, 3) for way in (1, -1)]


def front_kernel(
    small,
    n_batch,
    len_ref,
    group_ref,
    routes_ref,
    tok_ref,
    cot_ref,
    gain_one_ref,
    w_qkv_ref,
    w_proj_ref,
    gain_two_ref,
    w_in_ref,
    w_back_ref,
    qkv_hbm,
    ctx_hbm,
    lse_hbm,
    mid_hbm,
    g_hbm,
    x_hbm,
    wi_all,
    wb_all,
    offs_all,
    col_ref,
    qkv,
    ctx,
    lse,
    mid,
    g_sorted,
    x_sorted,
    held,
    stat,
    pos_ref,
    offs,
    wi_part,
    wb_part,
    local_sems,
    send_sems,
    recv_sems,
    hop_send,
    hop_recv,
    pass_send,
    pass_recv,
):
    batch, ffn = lax.axis_index("batch"), lax.axis_index("ffn")
    z, y = batch // 2, batch % 2
    near, far, cater = (batch, ffn ^ 1), (batch, ffn ^ 2), (batch, ffn ^ 3)
    across = (batch ^ 1, ffn)

    barrier = pltpu.get_barrier_semaphore()
    for device in [near, far, cater] + ([across] if small else []):
        pl.semaphore_signal(barrier, inc=1, device_id=device, device_id_type=MESH)
    if small:
        for way in (1, -1):

            @pl.when((z + way >= 0) & (z + way <= 3))
            def _(way=way):
                pl.semaphore_signal(
                    barrier, inc=1, device_id=(batch + 2 * way, ffn), device_id_type=MESH
                )

        inner = jnp.where((z == 0) | (z == 3), 1, 2)
        pl.semaphore_wait(barrier, 4 + inner)
    else:
        pl.semaphore_wait(barrier, 3)

    local_count = [0]
    waiting = []

    def local(src, dst):
        number = local_count[0]
        local_count[0] += 1
        copy = pltpu.make_async_copy(src, dst, local_sems.at[number])
        copy.start()
        waiting.append(copy)

    used = [0]

    def send(src, dst, device):
        number = used[0]
        used[0] += 1
        copy = pltpu.make_async_remote_copy(
            src_ref=src,
            dst_ref=dst,
            send_sem=send_sems.at[number],
            recv_sem=recv_sems.at[number],
            device_id=device,
            device_id_type=MESH,
        )
        copy.start()
        return copy

    part, whole = (wi_part, wb_part), (wi_all, wb_all)

    def valid(origin):
        return (origin >= 0) & (origin <= 3)

    def hop_copy(a, way, hop, origin, device):
        slot = whole[a].at[origin * 2 + y]
        number = HOPS.index((way, hop))
        return pltpu.make_async_remote_copy(
            src_ref=part[a] if hop == 1 else slot,
            dst_ref=slot,
            send_sem=hop_send.at[a, number],
            recv_sem=hop_recv.at[a, number],
            device_id=device,
            device_id_type=MESH,
        )

    def hop_go(a, hop, finish=False):
        for way in (1, -1):
            origin = z - way * (hop - 1)

            @pl.when(valid(origin) & valid(z + way))
            def _(way=way, origin=origin):
                copy = hop_copy(a, way, hop, origin, (batch + 2 * way, ffn))
                if finish:
                    copy.wait_send()
                else:
                    copy.start()

    def pass_copy(a, way, hop, origin, column):
        slot = whole[a].at[origin * 2 + column]
        number = HOPS.index((way, hop))
        return pltpu.make_async_remote_copy(
            src_ref=slot,
            dst_ref=slot,
            send_sem=pass_send.at[a, number],
            recv_sem=pass_recv.at[a, number],
            device_id=across,
            device_id_type=MESH,
        )

    def hop_came(a, hop):
        for way in (1, -1):
            origin = z - way * hop

            @pl.when(valid(origin))
            def _(way=way, origin=origin):
                hop_copy(a, way, hop, origin, (batch, ffn)).wait_recv()

        if hop < 3:
            hop_go(a, hop + 1)
        for way in (1, -1):
            origin = z - way * hop

            @pl.when(valid(origin))
            def _(way=way, origin=origin):
                pass_copy(a, way, hop, origin, y).start()

    own_over = []
    if small:
        rank = jnp.int32(0)
        for b in range(n_batch):
            same = (group_ref[b] == group_ref[batch]) & (b < batch)
            rank = rank + jnp.where(same, 1, 0)
        wi_part[...] = jnp.where(rank == 0, w_in_ref[0, :, 0:HALF], w_in_ref[0, :, HALF:FF_DEV])
        wb_part[...] = jnp.where(rank == 0, w_back_ref[0, 0:HALF, :], w_back_ref[0, HALF:FF_DEV, :])
        for a in range(2):
            hop_go(a, 1)
            own_over.append(send(part[a], whole[a].at[batch], across))
            local(part[a], whole[a].at[batch])

    exchanged = []
    route_rows(n_batch, group_ref, routes_ref, pos_ref, col_ref, offs)
    for slot, device in ((1, near), (2, far), (3, cater)):
        exchanged.append(send(offs, offs_all.at[pl.ds(slot, 1), :], device))
    local(offs, offs_all.at[pl.ds(0, 1), :])

    def sort_and_send(rows_ref, out_ref, out_hbm):
        pos = pos_ref[0:1, 0:ROWS]
        top = 0
        sent = []
        for size in SORT_TILES:
            want = top + lax.broadcasted_iota(I32, (size, ROWS), 0)
            hot = jnp.where(pos == want, 1.0, 0.0).astype(BF16)
            rows = pl.ds(top, size)
            out_ref[rows, :] = dot(hot, rows_ref[...]).astype(BF16)
            sent.append(send(out_ref.at[rows], out_hbm.at[2, rows], far))
            exchanged.append(send(out_ref.at[rows], out_hbm.at[1, rows], near))
            local(out_ref.at[rows], out_hbm.at[0, rows])
            top += size
        return sent

    def hand_on(sent, out_hbm):
        top = 0
        for copy, size in zip(sent, SORT_TILES):
            rows = pl.ds(top, size)
            copy.wait()
            exchanged.append(send(out_hbm.at[2, rows], out_hbm.at[3, rows], near))
            top += size

    held[1552:ROWS, :] = jnp.zeros((ROWS - 1552, D), BF16)
    held[0:TOK_DEV, :] = cot_ref[...]
    g_sent = sort_and_send(held, g_sorted, g_hbm)

    for i in range(3):
        top = min(TILE * (i + 1), TOK_DEV)
        rows = slice(TILE * i, top)
        normal, _ = norm_parts(tok_ref[rows, :].astype(F32))
        normed = (normal * gain_one_ref[...].reshape(1, D)).astype(BF16)
        qkv[rows, :] = dot(normed, w_qkv_ref[...]).astype(BF16)
    tail = slice(TOK_DEV, ROWS)
    qkv[tail, :] = jnp.zeros((ROWS - TOK_DEV, 3 * D), BF16)
    ctx[1552:ROWS, :] = jnp.zeros((ROWS - 1552, D), BF16)
    local(qkv, qkv_hbm)
    if small:
        hop_came(0, 1)

    @pl.loop(0, SEQ_DEV)
    def _(pair):
        attend_pair(pair, len_ref[pair], qkv, ctx, lse, stat)
        if small:

            @pl.when(pair == 1)
            def _():
                hop_came(1, 1)

            @pl.when(pair == 4)
            def _():
                hop_came(0, 2)

    local(ctx, ctx_hbm)
    local(lse, lse_hbm)
    for i in range(3):
        top = min(TILE * (i + 1), TOK_DEV)
        rows = slice(TILE * i, top)
        middle = tok_ref[rows, :].astype(F32) + dot(ctx[rows, :], w_proj_ref[...])
        mid[rows, :] = middle
        normal, _ = norm_parts(middle)
        held[rows, :] = (normal * gain_two_ref[...].reshape(1, D)).astype(BF16)
    local(mid, mid_hbm)
    if small:
        hop_came(1, 2)
    x_sent = sort_and_send(held, x_sorted, x_hbm)
    hand_on(g_sent, g_hbm)
    if small:
        hop_came(0, 3)
        hop_came(1, 3)
    hand_on(x_sent, x_hbm)
    for copy in exchanged + own_over:
        copy.wait()
    if small:
        for a in range(2):
            for hop in (1, 2, 3):
                hop_go(a, hop, finish=True)
            for way, hop in HOPS:
                origin = z - way * hop

                @pl.when(valid(origin))
                def _(a=a, way=way, hop=hop, origin=origin):
                    pass_copy(a, way, hop, origin, y).wait_send()
                    pass_copy(a, way, hop, origin, 1 - y).wait_recv()

    for copy in waiting:
        copy.wait()


def front(small, lengths, group_map, routes, tokens, *arrays):
    vmem = pl.BlockSpec(memory_space=pltpu.VMEM)
    any_space = pl.BlockSpec(memory_space=pl.ANY)
    tiles = len(SORT_TILES)
    copies = 6 * tiles + 2 + 3
    dma = pltpu.SemaphoreType.DMA
    return pl.pallas_call(
        functools.partial(front_kernel, small, group_map.shape[0]),
        out_shape=(
            jax.ShapeDtypeStruct((ROWS, 3 * D), BF16),
            jax.ShapeDtypeStruct((ROWS, D), BF16),
            jax.ShapeDtypeStruct((SEQ_DEV, 16, 384), F32),
            jax.ShapeDtypeStruct((TOK_DEV, D), F32),
            jax.ShapeDtypeStruct((4, SORTED, D), BF16),
            jax.ShapeDtypeStruct((4, SORTED, D), BF16),
            jax.ShapeDtypeStruct((8, D, HALF), BF16),
            jax.ShapeDtypeStruct((8, HALF, D), BF16),
            jax.ShapeDtypeStruct((4, 128), I32),
            jax.ShapeDtypeStruct((LANES, 128), I32),
        ),
        in_specs=[pl.BlockSpec(memory_space=pltpu.SMEM)] * 2 + [vmem] * (2 + len(arrays)),
        out_specs=(any_space,) * 8 + (vmem,) * 2,
        scratch_shapes=[
            pltpu.VMEM((ROWS, 3 * D), BF16),
            pltpu.VMEM((ROWS, D), BF16),
            pltpu.VMEM((SEQ_DEV, 16, 384), F32),
            pltpu.VMEM((TOK_DEV, D), F32),
            pltpu.VMEM((SORTED, D), BF16),
            pltpu.VMEM((SORTED, D), BF16),
            pltpu.VMEM((ROWS, D), BF16),
            pltpu.VMEM((384, 128), F32),
            pltpu.VMEM((1, LANES), I32),
            pltpu.VMEM((1, 128), I32),
            pltpu.VMEM((D, HALF), BF16),
            pltpu.VMEM((HALF, D), BF16),
            dma((2 * tiles + 7,)),
            dma((copies,)),
            dma((copies,)),
            dma((2, 6)),
            dma((2, 6)),
            dma((2, 6)),
            dma((2, 6)),
        ],
        compiler_params=params(collective_id=1, has_side_effects=True),
        name="front",
    )(lengths, group_map, routes, tokens, *arrays)


def gelu_both(u):
    below = 0.5 * (1.0 + lax.erf(u * (1.0 / math.sqrt(2.0))))
    density = jnp.exp(-0.5 * u * u) * (1.0 / math.sqrt(2.0 * math.pi))
    return u * below, below + u * density


MERGED = 2 * SORTED + 256
HEAD = 800
CHUNK = D // 8


def expert_kernel(sources, first, count, rows, carried, joined, cut, n_batch, offs_ref, group_ref, *refs):
    refs = list(refs)

    def take(count):
        head = refs[:count]
        del refs[:count]
        return head

    xs, gs = take(2), take(2)
    wi_hbm, wb_hbm = take(2)
    before = take(2) if carried else None
    earlier = take(4) if joined else None
    outs, gxs = take(2), take(2)
    dwi_ref, dwb_ref = take(2)
    xm, gm, wi, wb, acc_i, acc_b, hosts_ref, sems, join_sems = refs
    step = pl.program_id(0)
    expert = first + step
    slot = step % 2

    def join_copies():
        for number, (source, target) in enumerate(zip(earlier, outs + gxs)):
            yield pltpu.make_async_copy(source, target.at[0:HEAD, :], join_sems.at[number])

    def weight_copies(e, buffer, start):
        for p in range(2):
            host = hosts_ref[e * 2 + p]
            part = pl.ds(p * HALF, HALF)
            for number, source, target in (
                (0, wi_hbm.at[host], wi.at[buffer, :, part]),
                (1, wb_hbm.at[host], wb.at[buffer, part, :]),
            ):
                copy = pltpu.make_async_copy(source, target, sems.at[buffer, p, number])
                if start:
                    copy.start()
                else:
                    copy.wait()

    @pl.when(step == 0)
    def _():
        for e in range(EXPERTS):
            first_host, second_host = jnp.int32(n_batch), jnp.int32(n_batch)
            for b in reversed(range(n_batch)):
                hosting = group_ref[b] == e
                second_host = jnp.where(hosting, first_host, second_host)
                first_host = jnp.where(hosting, b, first_host)
            hosts_ref[2 * e] = first_host
            hosts_ref[2 * e + 1] = second_host
        weight_copies(first, 0, True)
        if joined:
            for copy in join_copies():
                copy.start()

    @pl.when(step + 1 < count)
    def _():
        weight_copies(expert + 1, 1 - slot, True)

    def blocks(count, act):
        @pl.loop(0, count)
        def _(i):
            act(pl.multiple_of(i * 16, 16))

    @pl.when((step == 0) & (rows == SORTED))
    def _():
        for s in range(2):
            live = pl.multiple_of(offs_ref[sources[s], EXPERTS], 16)

            def clear(at, s=s, live=live):
                spot = pl.ds(pl.multiple_of(live + at, 16), 16)
                outs[s][spot, :] = jnp.zeros((16, D), BF16)
                gxs[s][spot, :] = jnp.zeros((16, D), BF16)

            blocks((SORTED - live) // 16, clear)

    if carried:
        acc_i[...] = before[0][0].astype(F32)
        acc_b[...] = before[1][0].astype(F32)
    else:
        acc_i[...] = jnp.zeros_like(acc_i)
        acc_b[...] = jnp.zeros_like(acc_b)

    places = []
    total = jnp.int32(0)
    for s in range(2):
        begin = pl.multiple_of(offs_ref[sources[s], expert], 16)
        size = offs_ref[sources[s], expert + 1] - begin
        places.append((begin, total, size // 16))

        def gather(at, s=s, begin=begin, total=total):
            here = pl.ds(pl.multiple_of(begin + at, 16), 16)
            there = pl.ds(pl.multiple_of(total + at, 16), 16)
            xm[there, :] = xs[s][0, here, :]
            gm[there, :] = gs[s][0, here, :]

        blocks(size // 16, gather)
        total = total + size
    span = pl.multiple_of(total, 16)

    def blank(at):
        there = pl.ds(pl.multiple_of(span + at, 16), 16)
        xm[there, :] = jnp.zeros((16, D), BF16)
        gm[there, :] = jnp.zeros((16, D), BF16)

    blocks((256 - span % 256) // 16, blank)
    weight_copies(expert, slot, False)
    w_in, w_back = wi.at[slot], wb.at[slot]

    @pl.loop(0, (span + 255) // 256)
    def _(i):
        spot = pl.ds(pl.multiple_of(i * 256, 256), 256)
        x, g = xm[spot, :], gm[spot, :]
        inner = dot(x, w_in[...])
        hidden, slope = gelu_both(inner)
        hidden = hidden.astype(BF16)
        grad_hidden = dot(g, w_back[...], CONTRACT_LANES).astype(BF16)
        grad_inner = (grad_hidden.astype(F32) * slope).astype(BF16)
        xm[spot, :] = dot(hidden, w_back[...]).astype(BF16)
        gm[spot, :] = dot(grad_inner, w_in[...], CONTRACT_LANES).astype(BF16)
        acc_b[...] += dot(hidden, g, CONTRACT_ROWS)
        acc_i[...] += dot(x, grad_inner, CONTRACT_ROWS)

    if cut:
        y = lax.axis_index("batch") % 2
        for i, acc in enumerate((acc_i, acc_b)):
            for z in range(4):
                for ref, column in ((dwi_ref, 1 - y), (dwb_ref, y)):
                    part = pl.ds(pl.multiple_of((z * 2 + column) * CHUNK, 16), CHUNK)
                    ref[i, z] = acc[part, :].astype(BF16)
    else:
        dwi_ref[0] = acc_i[...].astype(BF16)
        dwb_ref[0] = acc_b[...].astype(BF16)
    if joined:

        @pl.when(step == 0)
        def _():
            for copy in join_copies():
                copy.wait()

    for s in range(2):
        begin, base, blocks_of = places[s]

        def hand_back(at, s=s, begin=begin, base=base):
            here = pl.ds(pl.multiple_of(begin + at, 16), 16)
            there = pl.ds(pl.multiple_of(base + at, 16), 16)
            outs[s][here, :] = xm[there, :]
            gxs[s][here, :] = gm[there, :]

        blocks(blocks_of, hand_back)


def experts(
    sources, offs, group_map, x, g, wi, wb, before=None, earlier=None, first=0, count=EXPERTS, cut=False
):
    rows = HEAD if cut else SORTED
    whole = once((rows, D))
    any_space = pl.BlockSpec(memory_space=pl.ANY)
    carried, joined = before is not None, earlier is not None
    out = jax.ShapeDtypeStruct((rows, D), BF16)

    def source(i):
        return pl.BlockSpec((1, rows, D), lambda e, *_: (i, 0, 0), pipeline_mode=pl.Buffered(1))

    carry = pl.BlockSpec((1, D, FF_DEV), lambda e, *_: (first + e, 0, 0))
    if cut:
        weight = once((2, 4, CHUNK, D))
        grad = jax.ShapeDtypeStruct((2, 4, CHUNK, D), BF16)
    else:
        weight = pl.BlockSpec((1, D, FF_DEV), lambda e, *_: (e, 0, 0))
        grad = jax.ShapeDtypeStruct((count, D, FF_DEV), BF16)
    picked = [source(i) for i in sources]
    kernel = functools.partial(
        expert_kernel, sources, first, count, rows, carried, joined, cut, group_map.shape[0]
    )
    return pl.pallas_call(
        kernel,
        grid_spec=pltpu.PrefetchScalarGridSpec(
            num_scalar_prefetch=2,
            grid=(count,),
            in_specs=picked
            + picked
            + [any_space] * 2
            + [carry] * (2 * carried)
            + [any_space] * (4 * joined),
            out_specs=[whole] * 4 + [weight] * 2,
            scratch_shapes=[
                pltpu.VMEM((MERGED, D), BF16),
                pltpu.VMEM((MERGED, D), BF16),
                pltpu.VMEM((2, D, FF_DEV), BF16),
                pltpu.VMEM((2, FF_DEV, D), BF16),
                pltpu.VMEM((D, FF_DEV), F32),
                pltpu.VMEM((FF_DEV, D), F32),
                pltpu.SMEM((2 * EXPERTS,), I32),
                pltpu.SemaphoreType.DMA((2, 2, 2)),
                pltpu.SemaphoreType.DMA((4,)),
            ],
        ),
        out_shape=(out,) * 4 + (grad,) * 2,
        compiler_params=params(),
        cost_estimate=cost(8 * count * SORTED * D * FF_DEV, 16 * SORTED * D),
        name="experts",
    )(offs, group_map, x, x, g, g, wi, wb, *(before or ()), *(earlier or ()))


def swap(rows, bit):
    pairs = [(f, f ^ bit) for f in range(4)]
    return lax.ppermute(rows, "ffn", pairs)


def tie(value, *others):
    return lax.optimization_barrier((value, *others))[0]


class Wire:
    def __init__(self, send_sems, recv_sems):
        self.send_sems, self.recv_sems, self.used = send_sems, recv_sems, 0

    def send(self, src, dst, device):
        number = self.used
        self.used += 1
        copy = pltpu.make_async_remote_copy(
            src_ref=src,
            dst_ref=dst,
            send_sem=self.send_sems.at[number],
            recv_sem=self.recv_sems.at[number],
            device_id=device,
            device_id_type=MESH,
        )
        copy.start()
        return copy


class Mover:
    def __init__(self, sems):
        self.sems, self.used = sems, 0

    def go(self, src, dst):
        number = self.used
        self.used += 1
        copy = pltpu.make_async_copy(src, dst, self.sems.at[number])
        copy.start()
        return copy


def greet(peers):
    barrier = pltpu.get_barrier_semaphore()
    for device in peers:
        pl.semaphore_signal(barrier, inc=1, device_id=device, device_id_type=MESH)
    pl.semaphore_wait(barrier, len(peers))


def wait_all(copies):
    for copy in copies:
        copy.wait()


def token_tiles():
    for i in range(3):
        yield slice(TILE * i, min(TILE * (i + 1), TOK_DEV))


def unsort(pos_col, src):
    want = lax.broadcasted_iota(I32, (pos_col.shape[0], SORTED), 1)
    hot = jnp.where(pos_col == want, 1.0, 0.0).astype(BF16)
    return dot(hot, src)


def attend_back_pair(pair, length, qkv_ref, gctx_ref, lse_ref, out_ref):
    start, skip = window(pair)
    start = pl.multiple_of(start, 16)
    row = lax.broadcasted_iota(I32, (WIN, 1), 0)
    mine = (row >= skip) & (row < skip + SEQ_LEN)
    bias = jnp.where((row >= skip) & (row < skip + PATCHES + length), 0.0, -1e30)
    lane = lax.broadcasted_iota(I32, (WIN, 128), 1)
    scale = jnp.asarray(HEAD_DIM**-0.5, BF16)
    @pl.loop(0, HEADS // 2)
    def _(hp):
        spots = [head_cols(hp, part) for part in range(3)]
        q, k, v = [qkv_ref[pl.ds(start, WIN), spot] for spot in spots]
        none = jnp.zeros_like(q)
        q = jnp.where(mine, q * scale, none)
        ks = k * scale
        go = jnp.where(mine, gctx_ref[pl.ds(start, WIN), spots[0]], none)
        low = lane < 64
        both_q = jnp.concatenate([jnp.where(low, q, none), jnp.where(low, none, q)], axis=0)
        both_go = jnp.concatenate([jnp.where(low, go, none), jnp.where(low, none, go)], axis=0)
        log_total = jnp.concatenate(
            [lse_ref[pair, pl.ds(hp * 2 + half, 1), 0:WIN] for half in range(2)], axis=1
        )
        probs = jnp.exp(dot(k, both_q, CONTRACT_LANES) + bias - log_total)
        grad_probs = dot(v, both_go, CONTRACT_LANES)
        delta = jnp.sum(probs * grad_probs, axis=0, keepdims=True)
        grad_scores = (probs * (grad_probs - delta)).astype(BF16)
        grad_v = dot(probs.astype(BF16), both_go)
        grad_k = dot(grad_scores, both_q)
        turned = dot(grad_scores, ks, CONTRACT_ROWS)
        grad_q = jnp.where(low, turned[0:WIN], turned[WIN : 2 * WIN])
        for spot, new in zip(spots, (grad_q, grad_k, grad_v)):
            old = out_ref[pl.ds(start, WIN), spot]
            out_ref[pl.ds(start, WIN), spot] = jnp.where(mine, new.astype(BF16), old)


TURNS = (2, 3, 1, 0)


def rear_kernel(
    small,
    len_ref,
    pos_ref,
    gain_one_ref,
    gain_two_ref,
    w_ref,
    lse_ref,
    gx0_hbm,
    gx1_hbm,
    gx2_hbm,
    mid_hbm,
    cot_hbm,
    ctx_hbm,
    qkv_hbm,
    tok_hbm,
    out1_hbm,
    out2_hbm,
    out3_hbm,
    dwi_hbm,
    dwb_hbm,
    first_came,
    first_own,
    gm_hbm,
    gq_hbm,
    dwq_hbm,
    dwp_hbm,
    dg_ref,
    share_hbm,
    near_hbm,
    far_hbm,
    wide,
    mid,
    cot,
    ctx,
    gctx,
    qkv,
    half_a,
    half_b,
    own_rows,
    came_y,
    came_z,
    acc,
    dwp,
    local_sems,
    send_sems,
    recv_sems,
    z_send,
    z_recv,
):
    batch, ffn = lax.axis_index("batch"), lax.axis_index("ffn")
    z, y = batch // 2, batch % 2
    near, far, across = (batch, ffn ^ 1), (batch, ffn ^ 2), (batch ^ 1, ffn)
    along = {k: (batch ^ (2 * k), ffn) for k in (1, 2, 3)}
    greet([near, far] + ([across] + list(along.values()) if small else []))
    wire, mover = Wire(send_sems, recv_sems), Mover(local_sems)

    parts_near = wire.send(gx1_hbm, wide.at[:, D : 2 * D], near)
    near_sent = wire.send(out3_hbm, half_b, near)
    half_in = mover.go(out2_hbm, half_a)
    over_y = {}
    own_in = {}
    if small:
        for turn in TURNS:
            there = pl.ds(pl.multiple_of(((z ^ turn) * 2 + 1 - y) * CHUNK, 16), CHUNK)
            over_y[turn] = [
                wire.send(grad.at[:, there, :], came_y.at[turn, i, 1:EXPERTS], across)
                for i, grad in enumerate((dwi_hbm, dwb_hbm))
            ]
    first_in = {}
    if small:
        for turn in TURNS:
            first_in[turn] = [
                mover.go(first_came.at[:, z ^ turn], came_y.at[turn, :, 0]),
                mover.go(first_own.at[:, z ^ turn], own_rows.at[turn, :, 0]),
            ]
    parts_in = [
        mover.go(part, wide.at[:, i * D : i * D + D])
        for i, part in ((0, gx0_hbm), (2, gx2_hbm))
    ]
    rows_in = [mover.go(mid_hbm, mid), mover.go(cot_hbm, cot), mover.go(ctx_hbm, ctx)]
    qkv_in = mover.go(qkv_hbm, qkv)
    if small:
        for turn in TURNS:
            here = pl.ds(pl.multiple_of(((z ^ turn) * 2 + y) * CHUNK, 16), CHUNK)
            own_in[turn] = [
                mover.go(grad.at[:, here, :], own_rows.at[turn, i, 1:EXPERTS])
                for i, grad in enumerate((dwi_hbm, dwb_hbm))
            ]
    sent = [wire.send(out1_hbm, near_hbm, near)]
    stored = []

    def z_copy(turn, i):
        return pltpu.make_async_remote_copy(
            src_ref=came_y.at[turn, i, 1:EXPERTS],
            dst_ref=came_z.at[turn - 1, i, 1:EXPERTS],
            send_sem=z_send.at[turn - 1, i],
            recv_sem=z_recv.at[turn - 1, i],
            device_id=along[turn],
            device_id_type=MESH,
        )

    def take_turn(turn, i):
        if not small:
            return
        over_y[turn][i].wait()
        own_in[turn][i].wait()
        for e in range(1, EXPERTS):
            came_y[turn, i, e] = (
                came_y[turn, i, e].astype(F32) + own_rows[turn, i, e].astype(F32)
            ).astype(BF16)
        if turn:
            z_copy(turn, i).start()

    first_z = []
    if small:
        for turn in TURNS:
            wait_all(first_in[turn])
            for i in range(2):
                came_y[turn, i, 0] = (
                    came_y[turn, i, 0].astype(F32) + own_rows[turn, i, 0].astype(F32)
                ).astype(BF16)
            if turn:
                first_z.append(
                    wire.send(came_y.at[turn, :, 0], came_z.at[turn - 1, :, 0], along[turn])
                )
    wait_all(parts_in + rows_in + [parts_near])
    top = 0
    for size in SORT_TILES:
        rows = slice(top, top + size)
        wide[rows, 0:D] = (
            wide[rows, 0:D].astype(F32)
            + wide[rows, D : 2 * D].astype(F32)
            + wide[rows, 2 * D : 3 * D].astype(F32)
        ).astype(BF16)
        top += size
    half_in.wait()
    near_sent.wait()
    half_a[...] = (half_a[...].astype(F32) + half_b[...].astype(F32)).astype(BF16)
    sent.append(wire.send(half_a, far_hbm, far))

    gctx[1552:ROWS, :] = jnp.zeros((ROWS - 1552, D), BF16)
    grad_gain = jnp.zeros((1, D), F32)
    for i, rows in enumerate(token_tiles()):
        grad_normed = unsort(pos_ref[rows, 0:1], wide[:, 0:D])
        normal, inverse = norm_parts(mid[rows, :])
        grad_gain = grad_gain + jnp.sum(grad_normed * normal, axis=0, keepdims=True)
        part = norm_pull(grad_normed, gain_two_ref[...].reshape(1, D), normal, inverse)
        grad_middle = cot[rows, :].astype(F32) + part
        mid[rows, :] = grad_middle
        low = grad_middle.astype(BF16)
        product = dot(ctx[rows, :], low, CONTRACT_ROWS)
        if i == 0:
            acc[...] = product
        elif i == 1:
            acc[...] += product
        else:
            dwp[...] = (acc[...] + product).astype(BF16)
        gctx[rows, :] = dot(low, w_ref[...], CONTRACT_LANES).astype(BF16)
        if i == 1:
            take_turn(2, 0)
            take_turn(2, 1)
    dg_ref[...] = grad_gain
    stored.append(mover.go(mid, gm_hbm))
    stored.append(mover.go(dwp, dwp_hbm))
    tok_in = mover.go(tok_hbm, cot)
    wide[1552:SORTED, :] = jnp.zeros((SORTED - 1552, 3 * D), BF16)
    qkv_in.wait()
    take_turn(3, 0)
    take_turn(3, 1)

    @pl.loop(0, SEQ_DEV)
    def _(pair):
        attend_back_pair(pair, len_ref[pair], qkv, gctx, lse_ref, wide)
        @pl.when(pair == 1)
        def _():
            take_turn(1, 0)
            take_turn(1, 1)

    stored.append(mover.go(wide.at[0:ROWS, :], gq_hbm))
    tok_in.wait()
    for rows in token_tiles():
        normal, _ = norm_parts(cot[rows, :].astype(F32))
        gctx[rows, :] = (normal * gain_one_ref[...].reshape(1, D)).astype(BF16)
    for i in range(3):
        part = slice(i * 256, i * 256 + 256)
        qkv[part, :] = dot(gctx[:, part], wide[0:ROWS, :], CONTRACT_ROWS).astype(BF16)
    stored.append(mover.go(qkv.at[0:D, :], dwq_hbm))
    if small:
        take_turn(0, 0)
        take_turn(0, 1)
        wait_all(first_z + [z_copy(turn, i) for turn in TURNS[:3] for i in range(2)])
        for i in range(2):
            for e in range(EXPERTS):
                total = came_y[0, i, e].astype(F32)
                for k in range(3):
                    total = total + came_z[k, i, e].astype(F32)
                came_y[0, i, e] = total.astype(BF16)
        stored.append(mover.go(came_y.at[0], share_hbm))
    wait_all(sent + stored)


def rear(small, lengths, pos_col, gain_one, gain_two, w_proj, lse, *arrays):
    vmem = pl.BlockSpec(memory_space=pltpu.VMEM)
    any_space = pl.BlockSpec(memory_space=pl.ANY)
    dma = pltpu.SemaphoreType.DMA
    copies = 15
    return pl.pallas_call(
        functools.partial(rear_kernel, small),
        out_shape=(
            jax.ShapeDtypeStruct((TOK_DEV, D), F32),
            jax.ShapeDtypeStruct((ROWS, 3 * D), BF16),
            jax.ShapeDtypeStruct((D, 3 * D), BF16),
            jax.ShapeDtypeStruct((D, D), BF16),
            jax.ShapeDtypeStruct((1, D), F32),
            jax.ShapeDtypeStruct((2, EXPERTS, CHUNK, D), BF16),
            jax.ShapeDtypeStruct((SORTED, D), BF16),
            jax.ShapeDtypeStruct((SORTED, D), BF16),
        ),
        in_specs=[pl.BlockSpec(memory_space=pltpu.SMEM)] + [vmem] * 5 + [any_space] * len(arrays),
        out_specs=(any_space,) * 4 + (vmem,) + (any_space,) * 3,
        scratch_shapes=[
            pltpu.VMEM((SORTED, 3 * D), BF16),
            pltpu.VMEM((TOK_DEV, D), F32),
            pltpu.VMEM((TOK_DEV, D), BF16),
            pltpu.VMEM((ROWS, D), BF16),
            pltpu.VMEM((ROWS, D), BF16),
            pltpu.VMEM((ROWS, 3 * D), BF16),
            pltpu.VMEM((SORTED, D), BF16),
            pltpu.VMEM((SORTED, D), BF16),
            pltpu.VMEM((4, 2, EXPERTS, CHUNK, D), BF16),
            pltpu.VMEM((4, 2, EXPERTS, CHUNK, D), BF16),
            pltpu.VMEM((3, 2, EXPERTS, CHUNK, D), BF16),
            pltpu.VMEM((D, D), F32),
            pltpu.VMEM((D, D), BF16),
            dma((32,)),
            dma((copies,)),
            dma((copies,)),
            dma((3, 2)),
            dma((3, 2)),
        ],
        compiler_params=params(collective_id=2, has_side_effects=True),
        name="rear",
    )(lengths, pos_col, gain_one, gain_two, w_proj, lse, *arrays)


ORDERS = (("x", "y", "z"), ("y", "x", "z")) * 2
WIDTHS = (1024, 1024, 512, 512)
LEFTS = (0, 1024, 2048, 2560)
SETS = ((0, 1), (2, 3))
WIDE = 4 * D
GAIN_ROWS = 8


def last_kernel(
    small,
    group_ref,
    pos_ref,
    gain_ref,
    w_ref,
    dg_two_ref,
    tok_hbm,
    gq_hbm,
    gm_hbm,
    mid_hbm,
    out0_hbm,
    out1_hbm,
    out2_hbm,
    dwq_hbm,
    dwp_hbm,
    share_hbm,
    ig_hbm,
    bo_hbm,
    sum_ref,
    gains_ref,
    pieces_ref,
    tok,
    gq,
    gm,
    mid,
    outs,
    share,
    stage,
    near_rows,
    held,
    came_z,
    came_xy,
    gain_in,
    local_sems,
    send_sems,
    recv_sems,
):
    batch, ffn = lax.axis_index("batch"), lax.axis_index("ffn")
    z, y, x, c = batch // 2, batch % 2, ffn // 2, ffn % 2
    place = {"x": x, "y": y, "z": z}
    mover = Mover(local_sems)

    def peer(axis, k=1):
        if axis == "c":
            return (batch, ffn ^ 1)
        if axis == "x":
            return (batch, ffn ^ 2)
        if axis == "y":
            return (batch ^ 1, ffn)
        return (batch ^ (2 * k), ffn)

    flying = ([], [])
    top = [0] * 4
    left = list(LEFTS)
    rows, cols = [384] * 4, list(WIDTHS)
    base = pl.multiple_of(c * 384, 16)
    if small:
        greet([peer("c"), peer("x")] + [(batch ^ j, ffn) for j in range(1, 8)])
        wire = Wire(send_sems, recv_sems)
        share_in = mover.go(share_hbm, share)
        give = pl.ds(pl.multiple_of((1 - c) * 384, 16), 384)
        keep = pl.ds(base, 384)
        pieces = (
            ((dwq_hbm, 0, 2048, 0),),
            ((dwq_hbm, 2048, 256, 2048), (dwp_hbm, 0, D, 3 * D)),
        )
        to_core, kept = [[], []], [[], []]
        for which in range(2):
            for ref, start, size, at in pieces[which]:
                lanes, spot = pl.ds(start, size), pl.ds(at, size)
                to_core[which].append(
                    wire.send(ref.at[give, lanes], near_rows.at[:, spot], peer("c"))
                )
                kept[which].append(mover.go(ref.at[keep, lanes], held.at[:, spot]))
    loads = [mover.go(tok_hbm, tok), mover.go(gq_hbm, gq), mover.go(gm_hbm, gm)]
    later = [mover.go(mid_hbm, mid)] + [
        mover.go(part, outs.at[i]) for i, part in enumerate((out0_hbm, out1_hbm, out2_hbm))
    ]
    handed = []

    def hand_out(i, *turns):
        for j in turns:
            handed.append(
                wire.send(stage.at[j, i], pieces_ref.at[batch, i], (batch ^ j, ffn))
            )

    if small:
        share_in.wait()
        for j in range(8):
            expert = group_ref[batch ^ j]
            for i in range(2):
                stage[j, i] = share[i, expert]
        hand_out(0, 4, 6, 5, 2)
        pieces_ref[batch] = stage[0]

    def core_done(which):
        wait_all(to_core[which] + kept[which])
        for i in SETS[which]:
            lanes = slice(LEFTS[i], LEFTS[i] + WIDTHS[i])
            held[:, lanes] = (
                held[:, lanes].astype(F32) + near_rows[:, lanes].astype(F32)
            ).astype(BF16)

    def sum_go(which, step):
        for i in SETS[which]:
            axis = ORDERS[i][step]
            quarter = WIDTHS[i] // 4
            if axis == "z":
                live = pl.ds(top[i], rows[i])
                for k in (2, 3, 1):
                    there = pl.ds(pl.multiple_of(left[i] + (z ^ k) * quarter, 128), quarter)
                    flying[which].append(
                        wire.send(
                            held.at[live, there],
                            came_z.at[i, k - 1, 0 : rows[i], 0:quarter],
                            peer("z", k),
                        )
                    )
            else:
                half = rows[i] // 2
                there = pl.ds(pl.multiple_of(top[i] + (1 - place[axis]) * half, 16), half)
                flying[which].append(
                    wire.send(
                        held.at[there, pl.ds(left[i], cols[i])],
                        came_xy.at[i, 0 if axis == "x" else 1, 0:half, 0 : cols[i]],
                        peer(axis),
                    )
                )

    def sum_done(which, step):
        wait_all(flying[which])
        flying[which].clear()
        for i in SETS[which]:
            axis = ORDERS[i][step]
            if axis == "z":
                cols[i] = WIDTHS[i] // 4
                left[i] = pl.multiple_of(left[i] + z * cols[i], 128)
                terms = [came_z[i, k, 0 : rows[i], 0 : cols[i]] for k in range(3)]
            else:
                rows[i] = rows[i] // 2
                top[i] = pl.multiple_of(top[i] + place[axis] * rows[i], 16)
                terms = [came_xy[i, 0 if axis == "x" else 1, 0 : rows[i], 0 : cols[i]]]
            spot = (pl.ds(top[i], rows[i]), pl.ds(left[i], cols[i]))
            total = held[spot].astype(F32)
            for term in terms:
                total = total + term.astype(F32)
            held[spot] = total.astype(BF16)
            if step == 2:
                lines = pl.ds(pl.multiple_of(base + top[i], 16), rows[i])
                sum_ref[lines, spot[1]] = total.astype(BF16)

    def spread_go(which, step):
        for i in SETS[which]:
            axis = ORDERS[i][step]
            mine = sum_ref.at[
                pl.ds(pl.multiple_of(base + top[i], 16), rows[i]), pl.ds(left[i], cols[i])
            ]
            for k in (2, 3, 1) if axis == "z" else (1,):
                flying[which].append(wire.send(mine, mine, peer(axis, k)))

    def spread_done(which, step):
        wait_all(flying[which])
        flying[which].clear()
        for i in SETS[which]:
            axis = ORDERS[i][step]
            if axis == "z":
                left[i] = LEFTS[i]
                cols[i] = WIDTHS[i]
            else:
                top[i] = top[i] - place[axis] * rows[i]
                rows[i] = rows[i] * 2

    def core_go(which):
        size = 2 * WIDTHS[SETS[which][0]]
        mine = sum_ref.at[pl.ds(base, 384), pl.ds(LEFTS[SETS[which][0]], size)]
        flying[which].append(wire.send(mine, mine, peer("c")))

    def gains_go(axis, slot):
        for k in (1, 2, 3) if axis == "z" else (1,):
            flying[0].append(wire.send(gains_ref, gain_in.at[slot + k - 1], peer(axis, k)))

    def gains_done(axis, slot):
        total = gains_ref[...]
        for k in (0, 1, 2) if axis == "z" else (0,):
            total = total + gain_in[slot + k]
        gains_ref[...] = total

    tiles = list(token_tiles())
    grad_gain = jnp.zeros((1, D), F32)
    stored = []

    def first_back(part):
        normal, inverse = norm_parts(tok[part, :].astype(F32))
        grad_normed = dot(gq[part, :], w_ref[...], CONTRACT_LANES)
        gain_part = jnp.sum(grad_normed * normal, axis=0, keepdims=True)
        pulled = norm_pull(grad_normed, gain_ref[...].reshape(1, D), normal, inverse)
        gm[part, :] = gm[part, :] + pulled
        stored.append(mover.go(gm.at[part], ig_hbm.at[part]))
        return gain_part

    def finish(part):
        mid[part, :] = mid[part, :] + unsort(pos_ref[part, 0:1], outs[0])
        stored.append(mover.go(mid.at[part], bo_hbm.at[part]))

    def finish_sums():
        wait_all(later)
        at = 0
        for size in SORT_TILES:
            part = slice(at, at + size)
            outs[0, part] = (
                outs[0, part].astype(F32) + outs[1, part].astype(F32) + outs[2, part].astype(F32)
            ).astype(BF16)
            at += size

    if small:
        for which in range(2):
            core_done(which)
            sum_go(which, 0)
    wait_all(loads)
    grad_gain = grad_gain + first_back(tiles[0])
    grad_gain = grad_gain + first_back(tiles[1])
    if small:
        for which in range(2):
            sum_done(which, 0)
            sum_go(which, 1)
    grad_gain = grad_gain + first_back(tiles[2])
    gains_ref[0:1, :] = grad_gain
    gains_ref[1:2, :] = dg_two_ref[...]
    gains_ref[2:GAIN_ROWS, :] = jnp.zeros((GAIN_ROWS - 2, D), F32)
    if small:
        gains_go("c", 0)
        for which in range(2):
            sum_done(which, 1)
            if which == 0:
                gains_done("c", 0)
                gains_go("x", 1)
            sum_go(which, 2)
    finish_sums()
    if small:
        for which in range(2):
            sum_done(which, 2)
            if which == 0:
                gains_done("x", 1)
                gains_go("y", 2)
            spread_go(which, 2)
    finish(tiles[0])
    finish(tiles[1])
    if small:
        for which in range(2):
            spread_done(which, 2)
            if which == 0:
                gains_done("y", 2)
                gains_go("z", 3)
            spread_go(which, 1)
        hand_out(0, 7, 3, 1)
        hand_out(1, 4, 6, 5, 7, 2, 3, 1)
    finish(tiles[2])
    if small:
        for which in range(2):
            spread_done(which, 1)
            if which == 0:
                gains_done("z", 3)
            spread_go(which, 0)
        for which in range(2):
            spread_done(which, 0)
            core_go(which)
        wait_all(flying[0] + flying[1] + handed)
    wait_all(stored)


def last(small, group_map, pos_col, gain_one, w_qkv, dg_two, *arrays):
    vmem = pl.BlockSpec(memory_space=pltpu.VMEM)
    any_space = pl.BlockSpec(memory_space=pl.ANY)
    dma = pltpu.SemaphoreType.DMA
    copies = 3 + 14 + 20 + 20 + 6 + 2
    extra = dict(collective_id=3, has_side_effects=True) if small else {}
    return pl.pallas_call(
        functools.partial(last_kernel, small),
        out_shape=(
            jax.ShapeDtypeStruct((TOK_DEV, D), F32),
            jax.ShapeDtypeStruct((TOK_DEV, D), F32),
            jax.ShapeDtypeStruct((D, WIDE), BF16),
            jax.ShapeDtypeStruct((GAIN_ROWS, D), F32),
            jax.ShapeDtypeStruct((8, 2, CHUNK, D), BF16),
        ),
        in_specs=[pl.BlockSpec(memory_space=pltpu.SMEM)] + [vmem] * 4 + [any_space] * len(arrays),
        out_specs=(any_space,) * 2 + (vmem,) * 3,
        scratch_shapes=[
            pltpu.VMEM((TOK_DEV, D), BF16),
            pltpu.VMEM((ROWS, 3 * D), BF16),
            pltpu.VMEM((TOK_DEV, D), F32),
            pltpu.VMEM((TOK_DEV, D), F32),
            pltpu.VMEM((3, SORTED, D), BF16),
            pltpu.VMEM((2, EXPERTS, CHUNK, D), BF16),
            pltpu.VMEM((8, 2, CHUNK, D), BF16),
            pltpu.VMEM((384, WIDE), BF16),
            pltpu.VMEM((384, WIDE), BF16),
            pltpu.VMEM((4, 3, 96, 256), BF16),
            pltpu.VMEM((4, 2, 192, 1024), BF16),
            pltpu.VMEM((6, GAIN_ROWS, D), F32),
            dma((20,)),
            dma((copies,)),
            dma((copies,)),
        ],
        compiler_params=params(**extra),
        name="last",
    )(group_map, pos_col, gain_one, w_qkv, dg_two, *arrays)


def close_kernel(
    sum_ref, gains_ref, pieces_ref, ig_ref, bo_ref, *outs
):
    qkv_ref, proj_ref, one_ref, two_ref, wi_ref, wb_ref, ig_out, bo_out = outs
    qkv_ref[...] = sum_ref[:, 0 : 3 * D].astype(F32)
    proj_ref[...] = sum_ref[:, 3 * D : WIDE].astype(F32)
    one_ref[...] = gains_ref[0:1, :].reshape(D)
    two_ref[...] = gains_ref[1:2, :].reshape(D)
    wi_ref[0] = pieces_ref[0, 0].astype(F32)
    wb_ref[0] = pieces_ref[0, 1].astype(F32)
    ig_out[...] = ig_ref[...]
    bo_out[...] = bo_ref[...]


def close(summed, gains, pieces, input_grad, block_out):
    row = pl.BlockSpec((CHUNK, D), lambda i: (i, 0))
    tokens = pl.BlockSpec((200, D), lambda i: (i, 0))
    weight = pl.BlockSpec((1, CHUNK, D), lambda i: (0, i, 0))
    rows = jax.ShapeDtypeStruct((TOK_DEV, D), F32)
    return pl.pallas_call(
        close_kernel,
        grid=(8,),
        out_shape=(
            jax.ShapeDtypeStruct((D, 3 * D), F32),
            jax.ShapeDtypeStruct((D, D), F32),
            jax.ShapeDtypeStruct((D,), F32),
            jax.ShapeDtypeStruct((D,), F32),
            jax.ShapeDtypeStruct((1, D, D), F32),
            jax.ShapeDtypeStruct((1, D, D), F32),
            rows,
            rows,
        ),
        in_specs=[
            pl.BlockSpec((CHUNK, WIDE), lambda i: (i, 0)),
            full((GAIN_ROWS, D)),
            pl.BlockSpec((1, 2, CHUNK, D), lambda i: (i, 0, 0, 0)),
            tokens,
            tokens,
        ],
        out_specs=(
            pl.BlockSpec((CHUNK, 3 * D), lambda i: (i, 0)),
            row,
            full((D,)),
            full((D,)),
            weight,
            weight,
            tokens,
            tokens,
        ),
        compiler_params=params(),
        name="close",
    )(summed, gains, pieces, input_grad, block_out)


def body(
    tokens,
    text_lengths,
    routes,
    group_map,
    gain_one,
    w_qkv,
    w_proj,
    gain_two,
    w_in,
    w_back,
    cotangent,
):
    n_batch = lax.axis_size("batch")
    own = lax.axis_index("batch")
    small = n_batch == 8
    routes_row = jnp.pad(routes.reshape(1, TOK_DEV), ((0, 0), (0, LANES - TOK_DEV)))
    qkv, context, lse, middle, g, x, wi_all, wb_all, offs, pos_col = front(
        small,
        text_lengths,
        group_map,
        routes_row,
        tokens,
        cotangent,
        gain_one,
        w_qkv,
        w_proj,
        gain_two,
        w_in,
        w_back,
    )
    if not small:
        own_expert = group_map[own]
        order = jnp.arange(n_batch, dtype=I32)
        rank = jnp.sum(jnp.where((group_map == own_expert) & (order < own), 1, 0))
        part = jnp.minimum(rank, 1)
        wi_part = lax.dynamic_slice(w_in[0], (0, part * HALF), (D, HALF))
        wb_part = lax.dynamic_slice(w_back[0], (part * HALF, 0), (HALF, D))
        wi_all = lax.all_gather(wi_part, "batch", axis=0)
        wb_all = lax.all_gather(wb_part, "batch", axis=0)

    def run(pair, x, *rest, **more):
        return experts(pair, offs, group_map, x, g, wi_all, wb_all, *rest, **more)

    def add(a, b):
        return (a.astype(F32) + b.astype(F32)).astype(BF16)

    out2, out3, gx2, gx3, dwi, dwb = run((2, 3), x)
    gx_half = add(gx2, swap(gx3, 1))
    gx_far = swap(gx_half, 2)
    x = tie(x, gx_half)
    if small:
        *earlier, going, staying = run((0, 1), x, (dwi, dwb), count=1, cut=True)
        came = lax.ppermute(going, "batch", [(b, b ^ 1) for b in range(8)])
        out0, out1, gx0, gx1, dwi, dwb = run((0, 1), x, (dwi, dwb), earlier, first=1, count=2)
    else:
        out0, out1, gx0, gx1, dwi, dwb = run((0, 1), x, (dwi, dwb))
        came = staying = jnp.zeros((2, 4, CHUNK, D), BF16)
    grad_middle, grad_qkv, dw_qkv, dw_proj, dg_two, share, out_near, out_far = rear(
        small,
        text_lengths,
        pos_col,
        gain_one,
        gain_two,
        w_proj,
        lse,
        gx0,
        gx1,
        gx_far,
        middle,
        cotangent,
        context,
        qkv,
        tokens,
        out1,
        out2,
        out3,
        dwi,
        dwb,
        came,
        staying,
    )
    input_grad, block_out, summed, gains, pieces = last(
        small,
        group_map,
        pos_col,
        gain_one,
        w_qkv,
        dg_two,
        tokens,
        grad_qkv,
        grad_middle,
        middle,
        out0,
        out_near,
        out_far,
        dw_qkv,
        dw_proj,
        share,
    )
    if small:
        summed_qkv, summed_proj, gain_a, gain_b, grad_w_in, grad_w_back, input_grad, block_out = close(
            summed, gains, pieces, input_grad, block_out
        )
        gains = (gain_a, gain_b)
    else:

        def settle_any(grad):
            share = lax.psum_scatter(grad, "batch", scatter_dimension=1, tiled=True)
            whole = lax.all_gather(share, "batch", axis=1, tiled=True)
            return lax.dynamic_index_in_dim(whole, own_expert, 0, keepdims=True).astype(F32)

        grad_w_in = settle_any(dwi)
        grad_w_back = settle_any(dwb)
        summed_qkv, summed_proj = lax.psum((dw_qkv, dw_proj), ("batch", "ffn"))
        gains = lax.psum(gains, ("batch", "ffn"))
    return (
        block_out,
        input_grad,
        gains[0],
        summed_qkv.astype(F32),
        summed_proj.astype(F32),
        gains[1],
        grad_w_in,
        grad_w_back,
    )


def solution(mesh):
    placed = (
        P(("batch", "ffn"), None),
        P(("batch", "ffn")),
        P(("batch", "ffn"), None),
        P(),
        P(),
        P(),
        P(),
        P(),
        P("batch", None, "ffn"),
        P("batch", "ffn", None),
        P(("batch", "ffn"), None),
    )
    return jax.shard_map(
        body,
        mesh=mesh,
        in_specs=placed,
        out_specs=(
            P(("batch", "ffn"), None),
            P(("batch", "ffn"), None),
            P(),
            P(),
            P(),
            P(),
            P("batch", None, "ffn"),
            P("batch", "ffn", None),
        ),
        check_vma=False,
    )
```

profile of v0, /device:TPU:0, one launch (start us, length us, event | category | flops | bytes accessed | tf_op | source)
XLA Modules:
  0.0 443.7 jit_solution(8505561250137348212)
XLA Ops:
  0.6 1.3 pad.4.routes_ref
  1.9 122.2 %front.1 = (bf16[1584,2304]{1,0:T(8,128)(2,1)}, bf16[1584,768]{1,0:T(8,128)(2,1)}, f32[6,16,384]{2,1,0:T(8,128)}, f32[1566,768]{1,0:T(8,128)}, bf16[4,1616,768]{...) custom-call(s32[6]{0:T(128)} %len_ref.3, ...), custom_call_target="tpu_custom_call" | custom-call | tf_op jit(solution)/shard_map/front/pallas_call | solution.py:423
  124.1 43.3 %experts.3 = (bf16[1616,768]{1,0:T(8,128)(2,1)}, bf16[1616,768]{1,0:T(8,128)(2,1)}, bf16[1616,768]{1,0:T(8,128)(2,1)}, bf16[1616,768]{1,0:T(8,128)(2,1)}, bf16[3...) custom-call(s32[4,128]{1,0:T(4,128)} %get-tuple-element.60.offs_ref, s32[8]{0:T(128)} %group_ref.9, ...), custom_call_target="tpu_custom_call" | custom-call | flops 22875734016 | bytes 19857408 | tf_op jit(solution)/shard_map/experts/pallas_call | solution.py:648
  167.4 0.4 collective-permute-start
  167.8 4.5 %collective-permute-done = bf16[1616,768]{1,0:T(8,128)(2,1)S(1)} collective-permute-done((bf16[1616,768]{1,0:T(8,128)(2,1)}, bf16[1616,768]{1,0:T(8,128)(2,1)S(1)}, u32[]{:S(2)}, u32[]{:S(2)}) %collective-permute-start) | collective-permute-done | bytes 2482208 | tf_op jit(solution)/shard_map/ppermute | solution.py:680
  172.4 2.4 add_convert_fusion
  174.8 1.1 collective-permute-start.1
  175.9 21.6 %experts.4 = (bf16[800,768]{1,0:T(8,128)(2,1)}, bf16[800,768]{1,0:T(8,128)(2,1)}, bf16[800,768]{1,0:T(8,128)(2,1)}, bf16[800,768]{1,0:T(8,128)(2,1)}, bf16[2,4,9...) custom-call(s32[4,128]{1,0:T(4,128)} %get-tuple-element.60.offs_ref, s32[8]{0:T(128)} %group_ref.9, ...), custom_call_target="tpu_custom_call" | custom-call | flops 7625244672 | bytes 19857408 | tf_op jit(solution)/shard_map/experts/pallas_call | solution.py:648
  197.5 1.6 collective-permute-start.2
  199.1 39.2 %experts.5 = (bf16[1616,768]{1,0:T(8,128)(2,1)}, bf16[1616,768]{1,0:T(8,128)(2,1)}, bf16[1616,768]{1,0:T(8,128)(2,1)}, bf16[1616,768]{1,0:T(8,128)(2,1)}, bf16[2...) custom-call(s32[4,128]{1,0:T(4,128)} %get-tuple-element.60.offs_ref, s32[8]{0:T(128)} %group_ref.9, ...), custom_call_target="tpu_custom_call" | custom-call | flops 15250489344 | bytes 19857408 | tf_op jit(solution)/shard_map/experts/pallas_call | solution.py:648
  238.3 0.0 collective-permute-done.2.first_came
  238.4 0.0 copy-start
  238.4 0.0 collective-permute-done.1.gx2_hbm
  238.4 1.0 copy-done
  239.4 81.8 %rear.1 = (f32[1566,768]{1,0:T(8,128)}, bf16[1584,2304]{1,0:T(8,128)(2,1)}, bf16[768,2304]{1,0:T(8,128)(2,1)}, bf16[768,768]{1,0:T(8,128)(2,1)}, f32[1,768]{1,0:...) custom-call(s32[6]{0:T(128)} %len_ref.3, ...), custom_call_target="tpu_custom_call" | custom-call | tf_op jit(solution)/shard_map/rear/pallas_call | solution.py:986
  321.2 107.4 %last.1 = (f32[1566,768]{1,0:T(8,128)}, f32[1566,768]{1,0:T(8,128)}, bf16[768,3072]{1,0:T(8,128)(2,1)}, f32[8,768]{1,0:T(8,128)}, bf16[8,2,96,768]{3,2,1,0:T(8,128)(2,1)}) custom-call(s32[8]{0:T(128)} %group_ref.9, s32[1664,128]{1,0:T(8,128)} %get-tuple-element.58.pos_ref, f32[768]{0:T(1024)} %gain_ref.1, bf16[768,2304]{1,0:T(8,128)(2,1)} %w_ref.3, ...), custom_call_target="tpu_custom_call" | custom-call | tf_op jit(solution)/shard_map/last/pallas_call | solution.py:1310
  428.6 14.6 %close.1 = (f32[768,2304]{1,0:T(8,128)}, f32[768,768]{1,0:T(8,128)}, f32[768]{0:T(1024)}, f32[768]{0:T(1024)}, f32[1,768,768]{2,1,0:T(8,128)}, /*index=5*/f32[1,...) custom-call(bf16[768,3072]{1,0:T(8,128)(2,1)} %get-tuple-element.95.sum_ref, ...), custom_call_target="tpu_custom_call" | custom-call | tf_op jit(solution)/shard_map/close/pallas_call | solution.py:1362
Async XLA Ops:
  167.4 5.0 %collective-permute-start = (bf16[1616,768]{1,0:T(8,128)(2,1)}, bf16[1616,768]{1,0:T(8,128)(2,1)S(1)}, u32[]{:S(2)}, u32[]{:S(2)}) collective-permute-start(bf16[1616,768]{1,0:T(8,128)(2,1)} %get-tuple-element.66), channel_id=1, source_target_pairs={{0,1},{1,0},{2,3},{3,2},{4,5},{5,4},{6,7},{7,6},{8,9},{9,8},{10,11... | collective-permute-start | bytes 7446536 | tf_op jit(solution)/shard_map/ppermute | solution.py:680
  174.8 63.6 %collective-permute-start.1 = (bf16[1616,768]{1,0:T(8,128)(2,1)S(1)}, bf16[1616,768]{1,0:T(8,128)(2,1)}, u32[]{:S(2)}, u32[]{:S(2)}) collective-permute-start(bf16[1616,768]{1,0:T(8,128)(2,1)S(1)} %add_convert_fusion), channel_id=1, source_target_pairs={{0,2},{1,3},{2,0},{3,1},{4,6},{5,7},{6,4},{7,5},{8,10},{9,11},{10,... | collective-permute-start | bytes 7446536 | tf_op jit(solution)/shard_map/ppermute | solution.py:680
  197.5 40.9 %collective-permute-start.2 = (bf16[2,4,96,768]{3,2,1,0:T(8,128)(2,1)}, bf16[2,4,96,768]{3,2,1,0:T(8,128)(2,1)S(1)}, u32[]{:S(2)}, u32[]{:S(2)}) collective-permute-start(bf16[2,4,96,768]{3,2,1,0:T(8,128)(2,1)} %get-tuple-element.84), channel_id=1, source_target_pairs={{0,4},{4,0},{8,12},{12,8},{16,20},{20,16},{24,28},{28,24},{1,5},{5... | collective-permute-start | bytes 3538952 | tf_op jit(solution)/shard_map/ppermute | solution.py:1450
  238.4 1.0 copy-start
where the time goes:
time: 452 us; the launch traced here: 444 us
  Pallas kernels  430 us (95%)
  waiting for transfers between devices  4.55 us (1%)
    pallas_call x1, Pallas kernels, front(): pl.pallas_call(functools.partial(front_kernel, small, group_map.shape[0])...  122 us
    pallas_call x1, Pallas kernels, last(): pl.pallas_call(functools.partial(last_kernel, small), out_shape=(jax.Shap...  107 us
    pallas_call x3, Pallas kernels, experts(): pl.pallas_call(kernel, grid_spec=pltpu.PrefetchScalarGridSpec(num_scalar_...  104 us
    pallas_call x1, Pallas kernels, rear(): pl.pallas_call(functools.partial(rear_kernel, small), out_shape=(jax.Shap...  81.8 us
    pallas_call x1, Pallas kernels, close(): pl.pallas_call(close_kernel, grid=(8,), out_shape=(jax.ShapeDtypeStruct((...  14.6 us
  transfers between devices with their start and end apart: 3, of which 1 were waited for; matrix products, arithmetic and copies ran while one was open for 0% of the time, Pallas kernels for 14%

commit v1 on v0

--- a/solution.py
+++ b/solution.py
@@ -898,10 +898,10 @@
                 came_y[turn, i, 0] = (
                     came_y[turn, i, 0].astype(F32) + own_rows[turn, i, 0].astype(F32)
                 ).astype(BF16)
-            if turn:
-                first_z.append(
-                    wire.send(came_y.at[turn, :, 0], came_z.at[turn - 1, :, 0], along[turn])
-                )
+        first_z = [
+            wire.send(came_y.at[turn, :, 0], came_z.at[turn - 1, :, 0], along[1])
+            for turn in (1, 3)
+        ]
     wait_all(parts_in + rows_in + [parts_near])
     top = 0
     for size in SORT_TILES:
@@ -935,6 +935,14 @@
         else:
             dwp[...] = (acc[...] + product).astype(BF16)
         gctx[rows, :] = dot(low, w_ref[...], CONTRACT_LANES).astype(BF16)
+        if small and i == 0:
+            wait_all(first_z)
+            for part_of in range(2):
+                for turn, slot in ((2, 2), (0, 0)):
+                    came_y[turn, part_of, 0] = (
+                        came_y[turn, part_of, 0].astype(F32) + came_z[slot, part_of, 0].astype(F32)
+                    ).astype(BF16)
+            first_z = [wire.send(came_y.at[2, :, 0], came_z.at[1, :, 0], along[2])]
         if i == 1:
             take_turn(2, 0)
             take_turn(2, 1)
@@ -971,7 +979,7 @@
         for i in range(2):
             for e in range(EXPERTS):
                 total = came_y[0, i, e].astype(F32)
-                for k in range(3):
+                for k in range(3) if e else (1,):
                     total = total + came_z[k, i, e].astype(F32)
                 came_y[0, i, e] = total.astype(BF16)
         stored.append(mover.go(came_y.at[0], share_hbm))

time: 452 us -> 457 us (1.011)
  Pallas kernels: 430 us -> 435 us
    pallas_call x1, Pallas kernels: 81.8 us -> 90.7 us  [rear(): pl.pallas_call(functools.partial(rear_kernel, small), out_shape=(jax.Shap...]
where the time goes in v1:
time: 457 us; the launch traced here: 449 us
  Pallas kernels  435 us (95%)
    pallas_call x1, Pallas kernels, front(): pl.pallas_call(functools.partial(front_kernel, small, group_map.shape[0])...  122 us
    pallas_call x3, Pallas kernels, experts(): pl.pallas_call(kernel, grid_spec=pltpu.PrefetchScalarGridSpec(num_scalar_...  104 us
    pallas_call x1, Pallas kernels, last(): pl.pallas_call(functools.partial(last_kernel, small), out_shape=(jax.Shap...  104 us
    pallas_call x1, Pallas kernels, rear(): pl.pallas_call(functools.partial(rear_kernel, small), out_shape=(jax.Shap...  90.7 us
    pallas_call x1, Pallas kernels, close(): pl.pallas_call(close_kernel, grid=(8,), out_shape=(jax.ShapeDtypeStruct((...  14.6 us
  transfers between devices with their start and end apart: 3, of which 1 were waited for; matrix products, arithmetic and copies ran while one was open for 0% of the time, Pallas kernels for 14%

profile of v1, /device:TPU:0, one launch (start us, length us, event | category | flops | bytes accessed | tf_op | source)
XLA Modules:
  0.0 448.9 jit_solution(13425317427015078411)
XLA Ops:
  0.6 1.3 pad.4.routes_ref
  1.9 122.2 %front.1 = (bf16[1584,2304]{1,0:T(8,128)(2,1)}, bf16[1584,768]{1,0:T(8,128)(2,1)}, f32[6,16,384]{2,1,0:T(8,128)}, f32[1566,768]{1,0:T(8,128)}, bf16[4,1616,768]{...) custom-call(s32[6]{0:T(128)} %len_ref.3, ...), custom_call_target="tpu_custom_call" | custom-call | tf_op jit(solution)/shard_map/front/pallas_call | solution.py:423
  124.1 43.3 %experts.3 = (bf16[1616,768]{1,0:T(8,128)(2,1)}, bf16[1616,768]{1,0:T(8,128)(2,1)}, bf16[1616,768]{1,0:T(8,128)(2,1)}, bf16[1616,768]{1,0:T(8,128)(2,1)}, bf16[3...) custom-call(s32[4,128]{1,0:T(4,128)} %get-tuple-element.60.offs_ref, s32[8]{0:T(128)} %group_ref.9, ...), custom_call_target="tpu_custom_call" | custom-call | flops 22875734016 | bytes 19857408 | tf_op jit(solution)/shard_map/experts/pallas_call | solution.py:648
  167.4 0.4 collective-permute-start
  167.8 4.5 %collective-permute-done = bf16[1616,768]{1,0:T(8,128)(2,1)S(1)} collective-permute-done((bf16[1616,768]{1,0:T(8,128)(2,1)}, bf16[1616,768]{1,0:T(8,128)(2,1)S(1)}, u32[]{:S(2)}, u32[]{:S(2)}) %collective-permute-start) | collective-permute-done | bytes 2482208 | tf_op jit(solution)/shard_map/ppermute | solution.py:680
  172.4 2.4 add_convert_fusion
  174.8 1.1 collective-permute-start.1
  175.9 21.6 %experts.4 = (bf16[800,768]{1,0:T(8,128)(2,1)}, bf16[800,768]{1,0:T(8,128)(2,1)}, bf16[800,768]{1,0:T(8,128)(2,1)}, bf16[800,768]{1,0:T(8,128)(2,1)}, bf16[2,4,9...) custom-call(s32[4,128]{1,0:T(4,128)} %get-tuple-element.60.offs_ref, s32[8]{0:T(128)} %group_ref.9, ...), custom_call_target="tpu_custom_call" | custom-call | flops 7625244672 | bytes 19857408 | tf_op jit(solution)/shard_map/experts/pallas_call | solution.py:648
  197.5 1.6 collective-permute-start.2
  199.1 39.2 %experts.5 = (bf16[1616,768]{1,0:T(8,128)(2,1)}, bf16[1616,768]{1,0:T(8,128)(2,1)}, bf16[1616,768]{1,0:T(8,128)(2,1)}, bf16[1616,768]{1,0:T(8,128)(2,1)}, bf16[2...) custom-call(s32[4,128]{1,0:T(4,128)} %get-tuple-element.60.offs_ref, s32[8]{0:T(128)} %group_ref.9, ...), custom_call_target="tpu_custom_call" | custom-call | flops 15250489344 | bytes 19857408 | tf_op jit(solution)/shard_map/experts/pallas_call | solution.py:648
  238.4 0.0 collective-permute-done.2.first_came
  238.4 0.0 copy-start
  238.4 0.0 collective-permute-done.1.gx2_hbm
  238.4 1.0 copy-done
  239.4 90.7 %rear.1 = (f32[1566,768]{1,0:T(8,128)}, bf16[1584,2304]{1,0:T(8,128)(2,1)}, bf16[768,2304]{1,0:T(8,128)(2,1)}, bf16[768,768]{1,0:T(8,128)(2,1)}, f32[1,768]{1,0:...) custom-call(s32[6]{0:T(128)} %len_ref.3, ...), custom_call_target="tpu_custom_call" | custom-call | tf_op jit(solution)/shard_map/rear/pallas_call | solution.py:994
  330.1 103.7 %last.1 = (f32[1566,768]{1,0:T(8,128)}, f32[1566,768]{1,0:T(8,128)}, bf16[768,3072]{1,0:T(8,128)(2,1)}, f32[8,768]{1,0:T(8,128)}, bf16[8,2,96,768]{3,2,1,0:T(8,128)(2,1)}) custom-call(s32[8]{0:T(128)} %group_ref.9, s32[1664,128]{1,0:T(8,128)} %get-tuple-element.58.pos_ref, f32[768]{0:T(1024)} %gain_ref.1, bf16[768,2304]{1,0:T(8,128)(2,1)} %w_ref.3, ...), custom_call_target="tpu_custom_call" | custom-call | tf_op jit(solution)/shard_map/last/pallas_call | solution.py:1318
  433.9 14.6 %close.1 = (f32[768,2304]{1,0:T(8,128)}, f32[768,768]{1,0:T(8,128)}, f32[768]{0:T(1024)}, f32[768]{0:T(1024)}, f32[1,768,768]{2,1,0:T(8,128)}, /*index=5*/f32[1,...) custom-call(bf16[768,3072]{1,0:T(8,128)(2,1)} %get-tuple-element.95.sum_ref, ...), custom_call_target="tpu_custom_call" | custom-call | tf_op jit(solution)/shard_map/close/pallas_call | solution.py:1370
Async XLA Ops:
  167.4 5.0 %collective-permute-start = (bf16[1616,768]{1,0:T(8,128)(2,1)}, bf16[1616,768]{1,0:T(8,128)(2,1)S(1)}, u32[]{:S(2)}, u32[]{:S(2)}) collective-permute-start(bf16[1616,768]{1,0:T(8,128)(2,1)} %get-tuple-element.66), channel_id=1, source_target_pairs={{0,1},{1,0},{2,3},{3,2},{4,5},{5,4},{6,7},{7,6},{8,9},{9,8},{10,11... | collective-permute-start | bytes 7446536 | tf_op jit(solution)/shard_map/ppermute | solution.py:680
  174.8 63.6 %collective-permute-start.1 = (bf16[1616,768]{1,0:T(8,128)(2,1)S(1)}, bf16[1616,768]{1,0:T(8,128)(2,1)}, u32[]{:S(2)}, u32[]{:S(2)}) collective-permute-start(bf16[1616,768]{1,0:T(8,128)(2,1)S(1)} %add_convert_fusion), channel_id=1, source_target_pairs={{0,2},{1,3},{2,0},{3,1},{4,6},{5,7},{6,4},{7,5},{8,10},{9,11},{10,... | collective-permute-start | bytes 7446536 | tf_op jit(solution)/shard_map/ppermute | solution.py:680
  197.5 40.9 %collective-permute-start.2 = (bf16[2,4,96,768]{3,2,1,0:T(8,128)(2,1)}, bf16[2,4,96,768]{3,2,1,0:T(8,128)(2,1)S(1)}, u32[]{:S(2)}, u32[]{:S(2)}) collective-permute-start(bf16[2,4,96,768]{3,2,1,0:T(8,128)(2,1)} %get-tuple-element.84), channel_id=1, source_target_pairs={{0,4},{4,0},{8,12},{12,8},{16,20},{20,16},{24,28},{28,24},{1,5},{5... | collective-permute-start | bytes 3538952 | tf_op jit(solution)/shard_map/ppermute | solution.py:1458
  238.4 1.0 copy-start

commit v2 on v0

--- a/solution.py
+++ b/solution.py
@@ -165,8 +165,8 @@
     tok_ref,
     cot_ref,
     gain_one_ref,
-    w_qkv_ref,
-    w_proj_ref,
+    w_qkv_hbm,
+    w_proj_hbm,
     gain_two_ref,
     w_in_ref,
     w_back_ref,
@@ -192,6 +192,9 @@
     offs,
     wi_part,
     wb_part,
+    w_qkv_ref,
+    w_proj_ref,
+    weight_sems,
     local_sems,
     send_sems,
     recv_sems,
@@ -222,6 +225,12 @@
     else:
         pl.semaphore_wait(barrier, 3)
 
+    weights_in = [
+        pltpu.make_async_copy(w_qkv_hbm, w_qkv_ref, weight_sems.at[0]),
+        pltpu.make_async_copy(w_proj_hbm, w_proj_ref, weight_sems.at[1]),
+    ]
+    for copy in weights_in:
+        copy.start()
     local_count = [0]
     waiting = []
 
@@ -351,6 +360,8 @@
     held[1552:ROWS, :] = jnp.zeros((ROWS - 1552, D), BF16)
     held[0:TOK_DEV, :] = cot_ref[...]
     g_sent = sort_and_send(held, g_sorted, g_hbm)
+    for copy in weights_in:
+        copy.wait()
 
     for i in range(3):
         top = min(TILE * (i + 1), TOK_DEV)
@@ -434,7 +445,10 @@
             jax.ShapeDtypeStruct((4, 128), I32),
             jax.ShapeDtypeStruct((LANES, 128), I32),
         ),
-        in_specs=[pl.BlockSpec(memory_space=pltpu.SMEM)] * 2 + [vmem] * (2 + len(arrays)),
+        in_specs=[pl.BlockSpec(memory_space=pltpu.SMEM)] * 2
+        + [vmem] * 4
+        + [any_space] * 2
+        + [vmem] * 3,
         out_specs=(any_space,) * 8 + (vmem,) * 2,
         scratch_shapes=[
             pltpu.VMEM((ROWS, 3 * D), BF16),
@@ -449,6 +463,9 @@
             pltpu.VMEM((1, 128), I32),
             pltpu.VMEM((D, HALF), BF16),
             pltpu.VMEM((HALF, D), BF16),
+            pltpu.VMEM((D, 3 * D), BF16),
+            pltpu.VMEM((D, D), BF16),
+            dma((2,)),
             dma((2 * tiles + 7,)),
             dma((copies,)),
             dma((copies,)),

time: 452 us -> 452 us (level)
  no operation moved by 1% of the time
where the time goes in v2:
time: 452 us; the launch traced here: 443 us
  Pallas kernels  430 us (95%)
  waiting for transfers between devices  4.55 us (1%)
    pallas_call x1, Pallas kernels, front(): pl.pallas_call(functools.partial(front_kernel, small, group_map.shape[0])...  121 us
    pallas_call x1, Pallas kernels, last(): pl.pallas_call(functools.partial(last_kernel, small), out_shape=(jax.Shap...  108 us
    pallas_call x3, Pallas kernels, experts(): pl.pallas_call(kernel, grid_spec=pltpu.PrefetchScalarGridSpec(num_scalar_...  104 us
    pallas_call x1, Pallas kernels, rear(): pl.pallas_call(functools.partial(rear_kernel, small), out_shape=(jax.Shap...  81.9 us
    pallas_call x1, Pallas kernels, close(): pl.pallas_call(close_kernel, grid=(8,), out_shape=(jax.ShapeDtypeStruct((...  14.6 us
  transfers between devices with their start and end apart: 3, of which 1 were waited for; matrix products, arithmetic and copies ran while one was open for 0% of the time, Pallas kernels for 14%

profile of v2, /device:TPU:0, one launch (start us, length us, event | category | flops | bytes accessed | tf_op | source)
XLA Modules:
  0.0 443.3 jit_solution(10653027194440051996)
XLA Ops:
  0.6 1.3 pad.4.routes_ref
  1.9 120.8 %front.1 = (bf16[1584,2304]{1,0:T(8,128)(2,1)}, bf16[1584,768]{1,0:T(8,128)(2,1)}, f32[6,16,384]{2,1,0:T(8,128)}, f32[1566,768]{1,0:T(8,128)}, bf16[4,1616,768]{...) custom-call(s32[6]{0:T(128)} %len_ref.3, ...), custom_call_target="tpu_custom_call" | custom-call | tf_op jit(solution)/shard_map/front/pallas_call | solution.py:434
  122.8 43.5 %experts.3 = (bf16[1616,768]{1,0:T(8,128)(2,1)}, bf16[1616,768]{1,0:T(8,128)(2,1)}, bf16[1616,768]{1,0:T(8,128)(2,1)}, bf16[1616,768]{1,0:T(8,128)(2,1)}, bf16[3...) custom-call(s32[4,128]{1,0:T(4,128)} %get-tuple-element.60.offs_ref, s32[8]{0:T(128)} %group_ref.9, ...), custom_call_target="tpu_custom_call" | custom-call | flops 22875734016 | bytes 19857408 | tf_op jit(solution)/shard_map/experts/pallas_call | solution.py:665
  166.3 0.4 collective-permute-start
  166.7 4.5 %collective-permute-done = bf16[1616,768]{1,0:T(8,128)(2,1)S(1)} collective-permute-done((bf16[1616,768]{1,0:T(8,128)(2,1)}, bf16[1616,768]{1,0:T(8,128)(2,1)S(1)}, u32[]{:S(2)}, u32[]{:S(2)}) %collective-permute-start) | collective-permute-done | bytes 2482208 | tf_op jit(solution)/shard_map/ppermute | solution.py:697
  171.3 2.4 add_convert_fusion
  173.7 1.1 collective-permute-start.1
  174.8 17.4 %experts.4 = (bf16[800,768]{1,0:T(8,128)(2,1)}, bf16[800,768]{1,0:T(8,128)(2,1)}, bf16[800,768]{1,0:T(8,128)(2,1)}, bf16[800,768]{1,0:T(8,128)(2,1)}, bf16[2,4,9...) custom-call(s32[4,128]{1,0:T(4,128)} %get-tuple-element.60.offs_ref, s32[8]{0:T(128)} %group_ref.9, ...), custom_call_target="tpu_custom_call" | custom-call | flops 7625244672 | bytes 19857408 | tf_op jit(solution)/shard_map/experts/pallas_call | solution.py:665
  192.2 1.6 collective-permute-start.2
  193.8 43.6 %experts.5 = (bf16[1616,768]{1,0:T(8,128)(2,1)}, bf16[1616,768]{1,0:T(8,128)(2,1)}, bf16[1616,768]{1,0:T(8,128)(2,1)}, bf16[1616,768]{1,0:T(8,128)(2,1)}, bf16[2...) custom-call(s32[4,128]{1,0:T(4,128)} %get-tuple-element.60.offs_ref, s32[8]{0:T(128)} %group_ref.9, ...), custom_call_target="tpu_custom_call" | custom-call | flops 15250489344 | bytes 19857408 | tf_op jit(solution)/shard_map/experts/pallas_call | solution.py:665
  237.3 0.0 collective-permute-done.2.first_came
  237.3 0.0 copy-start
  237.3 0.0 collective-permute-done.1.gx2_hbm
  237.4 1.0 copy-done
  238.4 81.9 %rear.1 = (f32[1566,768]{1,0:T(8,128)}, bf16[1584,2304]{1,0:T(8,128)(2,1)}, bf16[768,2304]{1,0:T(8,128)(2,1)}, bf16[768,768]{1,0:T(8,128)(2,1)}, f32[1,768]{1,0:...) custom-call(s32[6]{0:T(128)} %len_ref.3, ...), custom_call_target="tpu_custom_call" | custom-call | tf_op jit(solution)/shard_map/rear/pallas_call | solution.py:1003
  320.2 108.0 %last.1 = (f32[1566,768]{1,0:T(8,128)}, f32[1566,768]{1,0:T(8,128)}, bf16[768,3072]{1,0:T(8,128)(2,1)}, f32[8,768]{1,0:T(8,128)}, bf16[8,2,96,768]{3,2,1,0:T(8,128)(2,1)}) custom-call(s32[8]{0:T(128)} %group_ref.9, s32[1664,128]{1,0:T(8,128)} %get-tuple-element.58.pos_ref, f32[768]{0:T(1024)} %gain_ref.1, bf16[768,2304]{1,0:T(8,128)(2,1)} %w_ref.3, ...), custom_call_target="tpu_custom_call" | custom-call | tf_op jit(solution)/shard_map/last/pallas_call | solution.py:1327
  428.2 14.6 %close.1 = (f32[768,2304]{1,0:T(8,128)}, f32[768,768]{1,0:T(8,128)}, f32[768]{0:T(1024)}, f32[768]{0:T(1024)}, f32[1,768,768]{2,1,0:T(8,128)}, /*index=5*/f32[1,...) custom-call(bf16[768,3072]{1,0:T(8,128)(2,1)} %get-tuple-element.95.sum_ref, ...), custom_call_target="tpu_custom_call" | custom-call | tf_op jit(solution)/shard_map/close/pallas_call | solution.py:1379
Async XLA Ops:
  166.3 5.0 %collective-permute-start = (bf16[1616,768]{1,0:T(8,128)(2,1)}, bf16[1616,768]{1,0:T(8,128)(2,1)S(1)}, u32[]{:S(2)}, u32[]{:S(2)}) collective-permute-start(bf16[1616,768]{1,0:T(8,128)(2,1)} %get-tuple-element.66), channel_id=1, source_target_pairs={{0,1},{1,0},{2,3},{3,2},{4,5},{5,4},{6,7},{7,6},{8,9},{9,8},{10,11... | collective-permute-start | bytes 7446536 | tf_op jit(solution)/shard_map/ppermute | solution.py:697
  173.7 63.7 %collective-permute-start.1 = (bf16[1616,768]{1,0:T(8,128)(2,1)S(1)}, bf16[1616,768]{1,0:T(8,128)(2,1)}, u32[]{:S(2)}, u32[]{:S(2)}) collective-permute-start(bf16[1616,768]{1,0:T(8,128)(2,1)S(1)} %add_convert_fusion), channel_id=1, source_target_pairs={{0,2},{1,3},{2,0},{3,1},{4,6},{5,7},{6,4},{7,5},{8,10},{9,11},{10,... | collective-permute-start | bytes 7446536 | tf_op jit(solution)/shard_map/ppermute | solution.py:697
  192.2 45.1 %collective-permute-start.2 = (bf16[2,4,96,768]{3,2,1,0:T(8,128)(2,1)}, bf16[2,4,96,768]{3,2,1,0:T(8,128)(2,1)S(1)}, u32[]{:S(2)}, u32[]{:S(2)}) collective-permute-start(bf16[2,4,96,768]{3,2,1,0:T(8,128)(2,1)} %get-tuple-element.84), channel_id=1, source_target_pairs={{0,4},{4,0},{8,12},{12,8},{16,20},{20,16},{24,28},{28,24},{1,5},{5... | collective-permute-start | bytes 3538952 | tf_op jit(solution)/shard_map/ppermute | solution.py:1467
  237.3 1.0 copy-start
